TPU v7x, 512 devices: a whole 4x4x16 slice. The times are simulated.
512 devices in a mesh: expert: 4 (over z_hi, core), rep: 4 (over y), hid: 32 (over x, z_lo).
Axes of the slice: x: 4, y: 4, z: 16 (z_hi: 2, z_lo: 8; z = z_hi * 8 + z_lo), core: 2. Of those that a mesh axis runs over, the one named last changes fastest.
Arguments:
- tokens: bfloat16 [1024, 6144], P(('expert', 'hid'), 'rep'), may hold values from -6 to 6
- norm_gain: float32 [6144], P('rep'), may hold values from 0.25 to 1.75
- expert_ids: int32 [1024, 2], P(('expert', 'hid')), may hold values from 0 to 3, as said below
- slot_ids: int32 [1024, 2], P(('expert', 'hid')), may hold values from 0 to 4, as said below
- w_gate: bfloat16 [4, 6144, 8192], P('expert', 'rep', 'hid'), may hold values from -0.078125 to 0.078125
- w_up: bfloat16 [4, 6144, 8192], P('expert', 'rep', 'hid'), may hold values from -0.078125 to 0.078125
- grad_gate: bfloat16 [4, 640, 8192], P('expert', None, 'hid'), may hold values from -1.1953125 to 1.1953125
- grad_up: bfloat16 [4, 640, 8192], P('expert', None, 'hid'), may hold values from -1.1953125 to 1.1953125
Outputs:
- grad_w_gate: bfloat16 [4, 6144, 8192], P('expert', 'rep', 'hid')
- grad_w_up: bfloat16 [4, 6144, 8192], P('expert', 'rep', 'hid')
- grad_tokens: bfloat16 [1024, 6144], P(('expert', 'hid'), 'rep')
Inputs may be any that keep to these rules, and one draw needn't show every extreme that they name: `expert_ids`: each token names two different experts; among the 8 tokens of one block, no expert is named more than 5 times and some expert exactly 5 times. Within one block of 8 tokens, the pairs (expert_ids[t, k], slot_ids[t, k]) are all different.
All inputs are finite; a program needn't handle non-finite values.
Results may differ from a plain program's by a relative error of at most 0.0049.
Values may be sent and summed in bfloat16 or wider, within the bound.
No kernel may reach another device: no remote copies, remote signals or barrier semaphores. Data moves between devices by JAX's collectives and lax.ppermute only.
A program may use at most 64 MiB of HBM per device.

v0:
```python
import jax
import jax.numpy as jnp
from jax import lax
from jax.sharding import PartitionSpec as P

D = 6144


def copy_for_each(x, axis):
    size = lax.axis_size(axis)
    return lax.all_to_all(jnp.broadcast_to(x[None], (size, *x.shape)), axis, 0, 0, tiled=True)


def of_everyone(x, axis):
    return copy_for_each(x, axis).sum(axis=0)


def feature_total(partial_value):
    return of_everyone(partial_value, "rep")


def on_device(tokens, norm_gain, expert_ids, slot_ids, w_gate, w_up, grad_gate, grad_up):
    groups = lax.axis_size("expert")
    block_tokens = tokens.shape[0]
    slot_count = 5 * block_tokens // (2 * groups)
    values = tokens.astype(jnp.float32)
    square_sums = feature_total(jnp.sum(values * values, axis=1))
    inverse_rms = lax.rsqrt(square_sums / D + 1e-05)[:, None]
    scaled_in = values * inverse_rms
    normed = (scaled_in * norm_gain).astype(jnp.bfloat16)
    slot_code = expert_ids * slot_count + slot_ids
    codes_all = jnp.arange(groups * slot_count, dtype=jnp.int32)
    onehot = (
        (slot_code[:, 0][None, :] == codes_all[:, None])
        | (slot_code[:, 1][None, :] == codes_all[:, None])
    ).astype(jnp.bfloat16)
    feat_width = normed.shape[1]
    outgoing = (
        jnp.dot(onehot, normed, preferred_element_type=jnp.float32)
        .astype(jnp.bfloat16)
        .reshape(groups, slot_count, feat_width)
    )
    arrived = lax.all_to_all(outgoing, "expert", split_axis=0, concat_axis=0, tiled=True)
    own_rows = arrived.reshape(groups * slot_count, feat_width)
    gate_cot = grad_gate[0]
    up_cot = grad_up[0]
    row_contract = (((0,), (0,)), ((), ()))
    gathered = lax.all_gather(own_rows, "hid", axis=0, tiled=True)
    gate_part = gate_cot
    up_part = up_cot
    new_gate = lax.dot_general(
        gathered, gate_part, row_contract, preferred_element_type=jnp.float32
    )
    new_up = lax.dot_general(gathered, up_part, row_contract, preferred_element_type=jnp.float32)
    unit_contract = (((1,), (1,)), ((), ()))
    gate_part = gate_cot
    up_part = up_cot
    first_term = lax.dot_general(
        gate_part, w_gate[0], unit_contract, preferred_element_type=jnp.float32
    )
    summed = lax.psum_scatter(
        first_term
        + lax.dot_general(up_part, w_up[0], unit_contract, preferred_element_type=jnp.float32),
        "hid",
        scatter_dimension=0,
        tiled=True,
    )
    returned_rows = lax.all_to_all(
        summed.astype(jnp.bfloat16).reshape(groups, slot_count, feat_width),
        "expert",
        split_axis=0,
        concat_axis=0,
        tiled=True,
    )
    normed_grad = jnp.dot(
        onehot.T,
        returned_rows.reshape(groups * slot_count, feat_width),
        preferred_element_type=jnp.float32,
    )
    scaled = normed_grad * norm_gain
    dotted = feature_total(jnp.sum(scaled * scaled_in, axis=1)) / D
    grad_tokens = (inverse_rms * (scaled - scaled_in * dotted[:, None])).astype(jnp.bfloat16)
    return (new_gate.astype(jnp.bfloat16)[None], new_up.astype(jnp.bfloat16)[None], grad_tokens)


def solution(mesh):
    placed = (
        P(("expert", "hid"), "rep"),
        P("rep"),
        P(("expert", "hid"), None),
        P(("expert", "hid"), None),
        P("expert", "rep", "hid"),
        P("expert", "rep", "hid"),
        P("expert", None, "hid"),
        P("expert", None, "hid"),
    )
    return jax.shard_map(
        on_device,
        mesh=mesh,
        in_specs=placed,
        out_specs=(
            P("expert", "rep", "hid"),
            P("expert", "rep", "hid"),
            P(("expert", "hid"), "rep"),
        ),
        check_vma=False,
    )
```

profile of v0, /device:TPU:8, one launch (start us, length us, event | category | flops | bytes accessed | tf_op | source)
XLA Modules:
  0.0 289.3 jit_solution(9607621341677522654)
XLA Ops:
  7.2 0.0 copy-start
  7.2 0.9 fusion.18
  8.1 0.6 broadcast_in_dim.8
  8.7 9.0 %all-to-all-start = ((f32[4,1,8]{2,1,0:T(1,128)}), f32[4,1,8]{2,1,0:T(1,128)S(1)}, u32[]{:S(2)}, u32[]{:S(2)}) async-start(f32[4,1,8]{2,1,0:T(1,128)} %broadcast_in_dim.8), calls=%async_computation | async-start | bytes 4096 | tf_op jit(solution)/shard_map/all_to_all | solution.py:11
  17.7 0.0 copy-done
  17.7 0.0 copy-start.6
  17.7 0.0 copy-start.7
  17.7 0.0 copy-start.2
  17.7 0.0 copy-start.5
  17.7 0.0 copy-start.1
  17.7 0.0 copy-start.4
  17.7 3.6 %fusion.4 = f32[640,1536]{1,0:T(8,128)} fusion(bf16[1,1536,256]{2,1,0:T(8,128)(2,1)S(1)} %copy-done, bf16[1,640,256]{2,1,0:T(8,128)(2,1)} %param.14), kind=kOutput, calls=%fused_computation.8 | convolution fusion | flops 503316480 | bytes 5046272 | tf_op jit(solution)/shard_map/dot_general | solution.py:58
  21.4 0.0 copy-done.6
  21.4 0.0 copy-done.7
  21.4 0.0 all-to-all-done
  21.5 0.0 copy-done.2
  21.5 0.0 copy-done.5
  21.5 0.2 convolution_convert_fusion.2
  21.7 0.7 reshape.41
  22.4 11.0 %all-to-all-start.1 = ((bf16[4,5,1536]{2,1,0:T(8,128)(2,1)}), bf16[4,5,1536]{2,1,0:T(8,128)(2,1)S(1)}, u32[]{:S(2)}, u32[]{:S(2)}) async-start(bf16[4,5,1536]{2,1,0:T(8,128)(2,1)} %reshape.41), calls=%async_computation.1 | async-start | bytes 196608 | tf_op jit(solution)/shard_map/all_to_all | solution.py:43
  33.4 0.0 all-gather.3.cloned.1.call-start
  33.4 0.0 copy-done.1
  33.4 0.0 copy-done.4
  33.4 4.7 %convolution_add_fusion = f32[640,1536]{1,0:T(8,128)} fusion(f32[640,1536]{1,0:T(8,128)} %fusion.4, bf16[1,1536,256]{2,1,0:T(8,128)(2,1)S(1)} %copy-done.1, bf16[1,640,256]{2,1,0:T(8,128)(2,1)S(1)} %copy-done.4), kind=kOutput, calls=%fused_computation | convolution fusion | flops 504299520 | bytes 8978432 | tf_op jit(solution)/shard_map/dot_general | solution.py:63
  38.1 8.4 %all-to-all-done.1 = bf16[4,5,1536]{2,1,0:T(8,128)(2,1)S(1)} async-done(((bf16[4,5,1536]{2,1,0:T(8,128)(2,1)}), bf16[4,5,1536]{2,1,0:T(8,128)(2,1)S(1)}, u32[]{:S(2)}, u32[]{:S(2)}) %all-to-all-start.1) | async-done | bytes 61472 | tf_op jit(solution)/shard_map/all_to_all | solution.py:43
  46.5 0.7 reshape.45
  47.1 0.0 all-gather.3.cloned.1.call-update
  47.1 160.0 %fusion = f32[24,1536]{1,0:T(8,128)S(1)} fusion(f32[640,1536]{1,0:T(8,128)} %convolution_add_fusion), kind=kCustom, calls=%all-reduce-scatter | all-reduce-scatter fusion | flops 1179649 | bytes 4081664
  207.1 1.3 collective-permute-start.5
  208.5 1.3 collective-permute-start
  209.8 1.3 collective-permute-start.1
  211.1 1.3 collective-permute-start.2
  212.4 8.9 %collective-permute-start.3 = (bf16[24,1536]{1,0:T(8,128)(2,1)S(1)}, bf16[24,1536]{1,0:T(8,128)(2,1)S(1)}, u32[]{:S(2)}, u32[]{:S(2)}) collective-permute-start(bf16[24,1536]{1,0:T(8,128)(2,1)S(1)} %convert.10), channel_id=1, source_target_pairs={{0,4},{1,5},{2,6},{3,7},{4,8},{5,9},{6,10},{7,11},{8,12},{9,13},{1... | collective-permute-start | bytes 221192
  221.2 0.0 collective-permute-done.5
  221.3 1.3 collective-permute-start.4
  222.6 1.3 dynamic-slice.4
  224.5 0.0 collective-permute-done
  224.5 0.0 collective-permute-done.1
  224.5 0.0 collective-permute-done.2
  224.5 0.0 collective-permute-done.3
  224.5 0.0 collective-permute-done.4
  224.5 1.1 concatenate
  225.7 21.8 %all_to_all.22 = bf16[4,5,1536]{2,1,0:T(8,128)(2,1)S(1)} all-to-all(bf16[4,5,1536]{2,1,0:T(8,128)(2,1)S(1)} %reshape.43), channel_id=1, replica_groups=mesh['expert'=4,'rep'=4,'hid'=32] {'expert'}, dimensions={0} | all-to-all | bytes 122880 | tf_op jit(solution)/shard_map/all_to_all | solution.py:68
  247.5 0.0 copy-start.3
  247.6 0.3 fusion.14
  247.9 8.3 %all_to_all.23 = f32[4,1,8]{2,1,0:T(1,128)S(1)} all-to-all(f32[4,1,8]{2,1,0:T(1,128)S(1)} %broadcast_in_dim.11), channel_id=1, replica_groups=mesh['expert'=4,'rep'=4,'hid'=32] {'rep'}, dimensions={0} | all-to-all | bytes 256 | tf_op jit(solution)/shard_map/all_to_all | solution.py:11
  256.2 0.7 fusion.17
  256.9 19.5 %all-gather.3.cloned.1.call-done = bf16[32,20,1536]{2,1,0:T(8,128)(2,1)} async-done(((bf16[1,20,1536]{2,1,0:T(8,128)(2,1)}), bf16[32,20,1536]{2,1,0:T(8,128)(2,1)}) %all-gather.3.cloned.1.call-update) | async-done | bytes 1966096 | tf_op jit(solution)/shard_map/all_gather | solution.py:48
  276.4 2.6 reshape.46
  279.0 0.0 copy-done.3
  279.0 1.7 fusion.1
  280.7 1.7 fusion.2
  (12 shorter events, 0.2 us)
Async XLA Ops:
  7.2 10.5 %copy-start = (bf16[1,1536,256]{2,1,0:T(8,128)(2,1)S(1)}, bf16[1,1536,256]{2,1,0:T(8,128)(2,1)}, u32[]{:S(2)}) copy-start(bf16[1,1536,256]{2,1,0:T(8,128)(2,1)} %param.12) | copy-start | bytes 2359300
  8.7 12.7 %all-to-all-start = ((f32[4,1,8]{2,1,0:T(1,128)}), f32[4,1,8]{2,1,0:T(1,128)S(1)}, u32[]{:S(2)}, u32[]{:S(2)}) async-start(f32[4,1,8]{2,1,0:T(1,128)} %broadcast_in_dim.8), calls=%async_computation | async-start | bytes 4096 | tf_op jit(solution)/shard_map/all_to_all | solution.py:11
  17.7 3.7 %copy-start.6 = (s32[8,2]{0,1:T(2,128)S(1)}, s32[8,2]{0,1:T(2,128)}, u32[]{:S(2)}) copy-start(s32[8,2]{0,1:T(2,128)} %param.11) | copy-start | bytes 196
  17.7 3.7 %copy-start.7 = (s32[8,2]{0,1:T(2,128)S(1)}, s32[8,2]{0,1:T(2,128)}, u32[]{:S(2)}) copy-start(s32[8,2]{0,1:T(2,128)} %param.10) | copy-start | bytes 196
  17.7 3.8 %copy-start.2 = (bf16[8,1536]{1,0:T(8,128)(2,1)S(1)}, bf16[8,1536]{1,0:T(8,128)(2,1)}, u32[]{:S(2)}) copy-start(bf16[8,1536]{1,0:T(8,128)(2,1)} %param.8) | copy-start | bytes 73732
  17.7 3.8 %copy-start.5 = (f32[1536]{0:T(1024)S(1)}, f32[1536]{0:T(1024)}, u32[]{:S(2)}) copy-start(f32[1536]{0:T(1024)} %param.9) | copy-start | bytes 18436
  17.7 15.7 %copy-start.1 = (bf16[1,1536,256]{2,1,0:T(8,128)(2,1)S(1)}, bf16[1,1536,256]{2,1,0:T(8,128)(2,1)}, u32[]{:S(2)}) copy-start(bf16[1,1536,256]{2,1,0:T(8,128)(2,1)} %param.13) | copy-start | bytes 2359300
  17.7 15.7 %copy-start.4 = (bf16[1,640,256]{2,1,0:T(8,128)(2,1)S(1)}, bf16[1,640,256]{2,1,0:T(8,128)(2,1)}, u32[]{:S(2)}) copy-start(bf16[1,640,256]{2,1,0:T(8,128)(2,1)} %param.15) | copy-start | bytes 983044
  22.4 24.1 %all-to-all-start.1 = ((bf16[4,5,1536]{2,1,0:T(8,128)(2,1)}), bf16[4,5,1536]{2,1,0:T(8,128)(2,1)S(1)}, u32[]{:S(2)}, u32[]{:S(2)}) async-start(bf16[4,5,1536]{2,1,0:T(8,128)(2,1)} %reshape.41), calls=%async_computation.1 | async-start | bytes 196608 | tf_op jit(solution)/shard_map/all_to_all | solution.py:43
  33.4 243.1 %all-gather.3.cloned.1.call-start = ((), (), s32[]{:S(2)}) async-start(), calls=%async_computation.4 | async-start | bytes 2433024 | tf_op jit(solution)/shard_map/all_gather | solution.py:48
  207.1 14.1 %collective-permute-start.5 = (bf16[4,1536]{1,0:T(4,128)(2,1)S(1)}, bf16[4,1536]{1,0:T(4,128)(2,1)S(1)}, u32[]{:S(2)}, u32[]{:S(2)}) collective-permute-start(bf16[4,1536]{1,0:T(4,128)(2,1)S(1)} %slice.8), channel_id=1, source_target_pairs={{0,6},{1,7},{2,8},{3,9},{4,10},{5,11},{6,12},{7,13},{8,14},{9,15},... | collective-permute-start | bytes 36872
  208.5 16.0 %collective-permute-start = (bf16[24,1536]{1,0:T(8,128)(2,1)S(1)}, bf16[24,1536]{1,0:T(8,128)(2,1)S(1)}, u32[]{:S(2)}, u32[]{:S(2)}) collective-permute-start(bf16[24,1536]{1,0:T(8,128)(2,1)S(1)} %convert.10), channel_id=1, source_target_pairs={{0,1},{1,2},{2,3},{3,4},{4,5},{5,6},{6,7},{7,8},{8,9},{9,10},{10,1... | collective-permute-start | bytes 221192
  209.8 14.7 %collective-permute-start.1 = (bf16[24,1536]{1,0:T(8,128)(2,1)S(1)}, bf16[24,1536]{1,0:T(8,128)(2,1)S(1)}, u32[]{:S(2)}, u32[]{:S(2)}) collective-permute-start(bf16[24,1536]{1,0:T(8,128)(2,1)S(1)} %convert.10), channel_id=1, source_target_pairs={{0,2},{1,3},{2,4},{3,5},{4,6},{5,7},{6,8},{7,9},{8,10},{9,11},{10,... | collective-permute-start | bytes 221192
  211.1 13.4 %collective-permute-start.2 = (bf16[24,1536]{1,0:T(8,128)(2,1)S(1)}, bf16[24,1536]{1,0:T(8,128)(2,1)S(1)}, u32[]{:S(2)}, u32[]{:S(2)}) collective-permute-start(bf16[24,1536]{1,0:T(8,128)(2,1)S(1)} %convert.10), channel_id=1, source_target_pairs={{0,3},{1,4},{2,5},{3,6},{4,7},{5,8},{6,9},{7,10},{8,11},{9,12},{10... | collective-permute-start | bytes 221192
  212.4 12.1 %collective-permute-start.3 = (bf16[24,1536]{1,0:T(8,128)(2,1)S(1)}, bf16[24,1536]{1,0:T(8,128)(2,1)S(1)}, u32[]{:S(2)}, u32[]{:S(2)}) collective-permute-start(bf16[24,1536]{1,0:T(8,128)(2,1)S(1)} %convert.10), channel_id=1, source_target_pairs={{0,4},{1,5},{2,6},{3,7},{4,8},{5,9},{6,10},{7,11},{8,12},{9,13},{1... | collective-permute-start | bytes 221192
  221.3 3.3 %collective-permute-start.4 = (bf16[24,1536]{1,0:T(8,128)(2,1)S(1)}, bf16[24,1536]{1,0:T(8,128)(2,1)S(1)}, u32[]{:S(2)}, u32[]{:S(2)}) collective-permute-start(bf16[24,1536]{1,0:T(8,128)(2,1)S(1)} %convert.10), channel_id=1, source_target_pairs={{0,5},{1,6},{2,7},{3,8},{4,9},{5,10},{6,11},{7,12},{8,13},{9,14},{... | collective-permute-start | bytes 221192
  247.5 31.5 %copy-start.3 = (bf16[1,640,256]{2,1,0:T(8,128)(2,1)S(1)}, bf16[1,640,256]{2,1,0:T(8,128)(2,1)}, u32[]{:S(2)}) copy-start(bf16[1,640,256]{2,1,0:T(8,128)(2,1)} %param.14) | copy-start | bytes 983044
Sparse Core Ops, SparseCore 0:
  47.3 229.1 all-gather.2
where the time goes:
time: 290 us; the launch traced here: 289 us
  blocking collectives  190 us (66%)
  starting transfers between devices  35.3 us (12%)
  waiting for transfers between devices  28 us (10%)
  between operations  14.9 us (5%)
  matrix products  12.3 us (4%)
  local copies, waits for them, and re-layouts  7.02 us (2%)
    unnamed x1, blocking collectives  160 us
    all_to_all x1, blocking collectives, on_device(): lax.all_to_all(summed.astype(jnp.bfloat16).reshape(groups, slot_count, fe...  21.8 us
    all_gather x1, waiting for transfers between devices, on_device(): gathered = lax.all_gather(own_rows, 'hid', axis=0, tiled=True)  19.5 us
    unnamed x6, starting transfers between devices  15.3 us
    all_to_all x1, starting transfers between devices, on_device(): lax.all_to_all(outgoing, 'expert', split_axis=0, concat_axis=0, tiled=True)  11 us
    all_to_all x1, starting transfers between devices, copy_for_each(): lax.all_to_all(jnp.broadcast_to(x[None], (size, *x.shape)), axis, 0, 0, t...  8.98 us
    all_to_all x1, waiting for transfers between devices, on_device(): lax.all_to_all(outgoing, 'expert', split_axis=0, concat_axis=0, tiled=True)  8.38 us
    all_to_all x1, blocking collectives, copy_for_each(): lax.all_to_all(jnp.broadcast_to(x[None], (size, *x.shape)), axis, 0, 0, t...  8.3 us
  transfers between devices with their start and end apart: 9, of which 2 were waited for; matrix products, arithmetic and copies ran while one was open for 59% of the time, Pallas kernels for 0%

commit v1 on v0

--- a/solution.py
+++ b/solution.py
@@ -45,7 +45,9 @@
     gate_cot = grad_gate[0]
     up_cot = grad_up[0]
     row_contract = (((0,), (0,)), ((), ()))
-    gathered = lax.all_gather(own_rows, "hid", axis=0, tiled=True)
+    gathered = jnp.concatenate(
+        lax.all_to_all(jnp.stack(lax.axis_size("hid") * [own_rows], axis=0), "hid", 0, 0), axis=0
+    )
     gate_part = gate_cot
     up_part = up_cot
     new_gate = lax.dot_general(

time: 290 us -> 370 us (1.28)
  the two profiles are of different devices: /device:TPU:8 before, /device:TPU:32 now
where the time goes in v1:
time: 370 us
  blocking collectives  149 us (40%)
  waiting for transfers between devices  140 us (38%)
  starting transfers between devices  57.2 us (15%)
  matrix products  9.88 us (3%)
  local copies, waits for them, and re-layouts  9.69 us (3%)
    unnamed x1, blocking collectives  149 us
    all_to_all x1, waiting for transfers between devices, on_device(): lax.all_to_all(jnp.stack(lax.axis_size('hid') * [own_rows], axis=0), 'hid...  105 us
    unnamed x6, starting transfers between devices  21.7 us
    all_to_all x1, starting transfers between devices, on_device(): lax.all_to_all(jnp.stack(lax.axis_size('hid') * [own_rows], axis=0), 'hid...  13.9 us
    all_to_all x1, waiting for transfers between devices, on_device(): lax.all_to_all(outgoing, 'expert', split_axis=0, concat_axis=0, tiled=True)  12.6 us
    all_to_all x1, waiting for transfers between devices, on_device(): lax.all_to_all(summed.astype(jnp.bfloat16).reshape(groups, slot_count, fe...  12.1 us
    all_to_all x1, starting transfers between devices, on_device(): lax.all_to_all(summed.astype(jnp.bfloat16).reshape(groups, slot_count, fe...  9.61 us
    all_to_all x2, starting transfers between devices, copy_for_each(): lax.all_to_all(jnp.broadcast_to(x[None], (size, *x.shape)), axis, 0, 0, t...  8.64 us
  transfers between devices with their start and end apart: 11, of which 6 were waited for; matrix products, arithmetic and copies ran while one was open for 1% of the time, Pallas kernels for 0%

profile of v1, /device:TPU:32, one launch (start us, length us, event | category | flops | bytes accessed | tf_op | source)
XLA Modules:
  0.0 369.6 jit_solution(4485539712165382160)
XLA Ops:
  0.6 0.0 copy-start
  0.6 0.0 copy-start.2
  0.7 0.0 copy-start.5
  0.7 1.1 copy-done
  1.8 1.7 fusion.4
  3.5 0.0 copy-done.2
  3.5 0.0 copy-done.5
  3.5 2.6 convolution_add_fusion
  6.0 0.0 copy-start.3
  6.0 0.0 copy-start.8
  6.0 0.0 copy-start.9
  6.0 0.0 copy-start.7
  6.1 148.8 %fusion = f32[24,1536]{1,0:T(8,128)S(1)} fusion(f32[640,1536]{1,0:T(8,128)} %convolution_add_fusion), kind=kCustom, calls=%all-reduce-scatter | all-reduce-scatter fusion | flops 1179649 | bytes 4081664
  154.9 1.9 collective-permute-start
  156.8 1.3 collective-permute-start.1
  158.1 1.3 collective-permute-start.2
  159.4 7.5 %collective-permute-start.3 = (bf16[24,1536]{1,0:T(8,128)(2,1)S(1)}, bf16[24,1536]{1,0:T(8,128)(2,1)S(1)}, u32[]{:S(2)}, u32[]{:S(2)}) collective-permute-start(bf16[24,1536]{1,0:T(8,128)(2,1)S(1)} %convert.10), channel_id=1, source_target_pairs={{0,4},{1,5},{2,6},{3,7},{4,8},{5,9},{6,10},{7,11},{8,12},{9,13},{1... | collective-permute-start | bytes 221192
  166.9 6.4 %collective-permute-start.5 = (bf16[4,1536]{1,0:T(4,128)(2,1)S(1)}, bf16[4,1536]{1,0:T(4,128)(2,1)S(1)}, u32[]{:S(2)}, u32[]{:S(2)}) collective-permute-start(bf16[4,1536]{1,0:T(4,128)(2,1)S(1)} %slice.8), channel_id=1, source_target_pairs={{0,6},{1,7},{2,8},{3,9},{4,10},{5,11},{6,12},{7,13},{8,14},{9,15},... | collective-permute-start | bytes 36872
  173.3 0.0 copy-done.3
  173.3 0.1 fusion.18
  173.5 0.6 broadcast_in_dim.8
  174.0 5.4 %all-to-all-start = ((f32[4,1,8]{2,1,0:T(1,128)}), f32[4,1,8]{2,1,0:T(1,128)S(1)}, u32[]{:S(2)}, u32[]{:S(2)}) async-start(f32[4,1,8]{2,1,0:T(1,128)} %broadcast_in_dim.8), calls=%async_computation | async-start | bytes 4096 | tf_op jit(solution)/shard_map/all_to_all | solution.py:11
  179.5 0.0 copy-done.8
  179.5 0.0 copy-done.9
  179.5 1.3 dynamic-slice.4
  181.4 3.3 all-to-all-done
  184.7 0.0 collective-permute-done.5
  184.7 3.4 collective-permute-start.4
  188.1 0.0 collective-permute-done
  188.1 0.0 collective-permute-done.1
  188.1 0.0 collective-permute-done.2
  188.1 0.0 collective-permute-done.3
  188.1 2.6 collective-permute-done.4
  190.7 1.1 concatenate
  191.9 0.7 reshape.45
  192.6 9.6 %all-to-all-start.3 = ((bf16[4,5,1536]{2,1,0:T(8,128)(2,1)}), bf16[4,5,1536]{2,1,0:T(8,128)(2,1)S(1)}, u32[]{:S(2)}, u32[]{:S(2)}) async-start(bf16[4,5,1536]{2,1,0:T(8,128)(2,1)} %reshape.45), calls=%async_computation.3 | async-start | bytes 196608 | tf_op jit(solution)/shard_map/all_to_all | solution.py:70
  202.2 0.0 copy-done.7
  202.2 0.2 convolution_convert_fusion.2
  202.4 0.7 reshape.43
  203.1 12.1 %all-to-all-done.3 = bf16[4,5,1536]{2,1,0:T(8,128)(2,1)S(1)} async-done(((bf16[4,5,1536]{2,1,0:T(8,128)(2,1)}), bf16[4,5,1536]{2,1,0:T(8,128)(2,1)S(1)}, u32[]{:S(2)}, u32[]{:S(2)}) %all-to-all-start.3) | async-done | bytes 61472 | tf_op jit(solution)/shard_map/all_to_all | solution.py:70
  215.2 3.3 all-to-all-start.1
  218.5 0.3 fusion.14
  218.9 12.6 %all-to-all-done.1 = bf16[4,5,1536]{2,1,0:T(8,128)(2,1)S(1)} async-done(((bf16[4,5,1536]{2,1,0:T(8,128)(2,1)}), bf16[4,5,1536]{2,1,0:T(8,128)(2,1)S(1)}, u32[]{:S(2)}, u32[]{:S(2)}) %all-to-all-start.1) | async-done | bytes 61472 | tf_op jit(solution)/shard_map/all_to_all | solution.py:43
  231.5 0.6 broadcast_in_dim.11
  232.1 3.2 all-to-all-start.4
  235.3 5.1 %all-to-all-done.4 = f32[4,1,8]{2,1,0:T(1,128)S(1)} async-done(((f32[4,1,8]{2,1,0:T(1,128)}), f32[4,1,8]{2,1,0:T(1,128)S(1)}, u32[]{:S(2)}, u32[]{:S(2)}) %all-to-all-start.4) | async-done | bytes 160 | tf_op jit(solution)/shard_map/all_to_all | solution.py:11
  240.5 1.6 stack.3
  242.0 13.9 %all-to-all-start.2 = ((bf16[32,20,1536]{2,1,0:T(8,128)(2,1)}), bf16[32,20,1536]{2,1,0:T(8,128)(2,1)S(1)}, u32[]{:S(2)}, u32[]{:S(2)}) async-start(bf16[32,20,1536]{2,1,0:T(8,128)(2,1)} %stack.3), calls=%async_computation.2 | async-start | bytes 4718592 | tf_op jit(solution)/shard_map/all_to_all | solution.py:49
  255.9 0.0 copy-start.4
  255.9 0.5 reduce_sum.39
  256.4 0.7 broadcast_multiply_fusion
  257.1 0.7 fusion.17
  257.8 104.7 %all-to-all-done.2 = bf16[32,20,1536]{2,1,0:T(8,128)(2,1)S(1)} async-done(((bf16[32,20,1536]{2,1,0:T(8,128)(2,1)}), bf16[32,20,1536]{2,1,0:T(8,128)(2,1)S(1)}, u32[]{:S(2)}, u32[]{:S(2)}) %all-to-all-start.2) | async-done | bytes 1966112 | tf_op jit(solution)/shard_map/all_to_all | solution.py:49
  362.5 2.0 reshape.44
  364.5 0.0 copy-done.4
  364.5 0.0 copy-start.1
  364.5 0.0 copy-start.6
  364.5 3.4 fusion.1
  367.9 0.0 copy-done.1
  367.9 0.0 copy-done.6
  367.9 1.7 fusion.2
  (9 shorter events, 0.1 us)
Async XLA Ops:
  0.6 1.1 copy-start
  0.6 2.8 copy-start.2
  0.7 2.8 copy-start.5
  6.0 167.3 %copy-start.3 = (bf16[8,1536]{1,0:T(8,128)(2,1)S(1)}, bf16[8,1536]{1,0:T(8,128)(2,1)}, u32[]{:S(2)}) copy-start(bf16[8,1536]{1,0:T(8,128)(2,1)} %param.8) | copy-start | bytes 73732
  6.0 173.4 %copy-start.8 = (s32[8,2]{0,1:T(2,128)S(1)}, s32[8,2]{0,1:T(2,128)}, u32[]{:S(2)}) copy-start(s32[8,2]{0,1:T(2,128)} %param.11) | copy-start | bytes 196
  6.0 173.4 %copy-start.9 = (s32[8,2]{0,1:T(2,128)S(1)}, s32[8,2]{0,1:T(2,128)}, u32[]{:S(2)}) copy-start(s32[8,2]{0,1:T(2,128)} %param.10) | copy-start | bytes 196
  6.0 196.1 %copy-start.7 = (f32[1536]{0:T(1024)S(1)}, f32[1536]{0:T(1024)}, u32[]{:S(2)}) copy-start(f32[1536]{0:T(1024)} %param.9) | copy-start | bytes 18436
  154.9 33.2 %collective-permute-start = (bf16[24,1536]{1,0:T(8,128)(2,1)S(1)}, bf16[24,1536]{1,0:T(8,128)(2,1)S(1)}, u32[]{:S(2)}, u32[]{:S(2)}) collective-permute-start(bf16[24,1536]{1,0:T(8,128)(2,1)S(1)} %convert.10), channel_id=1, source_target_pairs={{0,1},{1,2},{2,3},{3,4},{4,5},{5,6},{6,7},{7,8},{8,9},{9,10},{10,1... | collective-permute-start | bytes 221192
  156.8 31.3 %collective-permute-start.1 = (bf16[24,1536]{1,0:T(8,128)(2,1)S(1)}, bf16[24,1536]{1,0:T(8,128)(2,1)S(1)}, u32[]{:S(2)}, u32[]{:S(2)}) collective-permute-start(bf16[24,1536]{1,0:T(8,128)(2,1)S(1)} %convert.10), channel_id=1, source_target_pairs={{0,2},{1,3},{2,4},{3,5},{4,6},{5,7},{6,8},{7,9},{8,10},{9,11},{10,... | collective-permute-start | bytes 221192
  158.1 30.0 %collective-permute-start.2 = (bf16[24,1536]{1,0:T(8,128)(2,1)S(1)}, bf16[24,1536]{1,0:T(8,128)(2,1)S(1)}, u32[]{:S(2)}, u32[]{:S(2)}) collective-permute-start(bf16[24,1536]{1,0:T(8,128)(2,1)S(1)} %convert.10), channel_id=1, source_target_pairs={{0,3},{1,4},{2,5},{3,6},{4,7},{5,8},{6,9},{7,10},{8,11},{9,12},{10... | collective-permute-start | bytes 221192
  159.4 28.7 %collective-permute-start.3 = (bf16[24,1536]{1,0:T(8,128)(2,1)S(1)}, bf16[24,1536]{1,0:T(8,128)(2,1)S(1)}, u32[]{:S(2)}, u32[]{:S(2)}) collective-permute-start(bf16[24,1536]{1,0:T(8,128)(2,1)S(1)} %convert.10), channel_id=1, source_target_pairs={{0,4},{1,5},{2,6},{3,7},{4,8},{5,9},{6,10},{7,11},{8,12},{9,13},{1... | collective-permute-start | bytes 221192
  166.9 17.8 %collective-permute-start.5 = (bf16[4,1536]{1,0:T(4,128)(2,1)S(1)}, bf16[4,1536]{1,0:T(4,128)(2,1)S(1)}, u32[]{:S(2)}, u32[]{:S(2)}) collective-permute-start(bf16[4,1536]{1,0:T(4,128)(2,1)S(1)} %slice.8), channel_id=1, source_target_pairs={{0,6},{1,7},{2,8},{3,9},{4,10},{5,11},{6,12},{7,13},{8,14},{9,15},... | collective-permute-start | bytes 36872
  174.0 10.6 %all-to-all-start = ((f32[4,1,8]{2,1,0:T(1,128)}), f32[4,1,8]{2,1,0:T(1,128)S(1)}, u32[]{:S(2)}, u32[]{:S(2)}) async-start(f32[4,1,8]{2,1,0:T(1,128)} %broadcast_in_dim.8), calls=%async_computation | async-start | bytes 4096 | tf_op jit(solution)/shard_map/all_to_all | solution.py:11
  184.7 6.1 %collective-permute-start.4 = (bf16[24,1536]{1,0:T(8,128)(2,1)S(1)}, bf16[24,1536]{1,0:T(8,128)(2,1)S(1)}, u32[]{:S(2)}, u32[]{:S(2)}) collective-permute-start(bf16[24,1536]{1,0:T(8,128)(2,1)S(1)} %convert.10), channel_id=1, source_target_pairs={{0,5},{1,6},{2,7},{3,8},{4,9},{5,10},{6,11},{7,12},{8,13},{9,14},{... | collective-permute-start | bytes 221192
  192.6 22.6 %all-to-all-start.3 = ((bf16[4,5,1536]{2,1,0:T(8,128)(2,1)}), bf16[4,5,1536]{2,1,0:T(8,128)(2,1)S(1)}, u32[]{:S(2)}, u32[]{:S(2)}) async-start(bf16[4,5,1536]{2,1,0:T(8,128)(2,1)} %reshape.45), calls=%async_computation.3 | async-start | bytes 196608 | tf_op jit(solution)/shard_map/all_to_all | solution.py:70
  215.2 16.3 %all-to-all-start.1 = ((bf16[4,5,1536]{2,1,0:T(8,128)(2,1)}), bf16[4,5,1536]{2,1,0:T(8,128)(2,1)S(1)}, u32[]{:S(2)}, u32[]{:S(2)}) async-start(bf16[4,5,1536]{2,1,0:T(8,128)(2,1)} %reshape.43), calls=%async_computation.1 | async-start | bytes 196608 | tf_op jit(solution)/shard_map/all_to_all | solution.py:43
  232.1 8.4 %all-to-all-start.4 = ((f32[4,1,8]{2,1,0:T(1,128)}), f32[4,1,8]{2,1,0:T(1,128)S(1)}, u32[]{:S(2)}, u32[]{:S(2)}) async-start(f32[4,1,8]{2,1,0:T(1,128)} %broadcast_in_dim.11), calls=%async_computation.4 | async-start | bytes 4096 | tf_op jit(solution)/shard_map/all_to_all | solution.py:11
  242.0 120.4 %all-to-all-start.2 = ((bf16[32,20,1536]{2,1,0:T(8,128)(2,1)}), bf16[32,20,1536]{2,1,0:T(8,128)(2,1)S(1)}, u32[]{:S(2)}, u32[]{:S(2)}) async-start(bf16[32,20,1536]{2,1,0:T(8,128)(2,1)} %stack.3), calls=%async_computation.2 | async-start | bytes 4718592 | tf_op jit(solution)/shard_map/all_to_all | solution.py:49
  255.9 108.6 %copy-start.4 = (bf16[1,640,256]{2,1,0:T(8,128)(2,1)S(1)}, bf16[1,640,256]{2,1,0:T(8,128)(2,1)}, u32[]{:S(2)}) copy-start(bf16[1,640,256]{2,1,0:T(8,128)(2,1)} %param.14) | copy-start | bytes 983044
  364.5 3.4 copy-start.1
  364.5 3.4 copy-start.6
